TPU v7x, 32 devices: a whole 2x2x4 slice. The times are simulated.
32 devices in a mesh: groups: 2 (over x), replica: 8 (over z, y), channel: 2 (over core).
Axes of the slice: x: 2, y: 2, z: 4, core: 2. Of those that a mesh axis runs over, the one named last changes fastest.
Arguments:
- queries: bfloat16 [16, 2, 32, 4096], P(('groups', 'replica'), None, None, 'channel'), parts along dimension 0, may hold values from -360 to 360
- new_kv: bfloat16 [16, 2, 32, 1024], P(('groups', 'replica'), None, None, 'channel'), parts along dimension 0, may hold values from -6 to 6
- cached_lookup_pairs: bfloat16 [16, 1024, 1024], P(('groups', 'replica'), None, 'channel'), parts along dimension 0, may hold values from -6 to 6
- prefix_ssm: bfloat16 [16, 16, 8192], P(('groups', 'replica'), None, 'channel'), parts along dimension 0, may hold values from -6 to 6
- prefix_conv: bfloat16 [16, 3, 8192], P(('groups', 'replica'), None, 'channel'), parts along dimension 0, may hold values from -6 to 6
- pool_kv: bfloat16 [16, 4, 256, 1024], P(('groups', 'replica'), None, None, 'channel'), parts along dimension 0, may hold values from -6 to 6
- pool_ssm: bfloat16 [16, 16, 8192], P(('groups', 'replica'), None, 'channel'), parts along dimension 0, may hold values from -6 to 6
- pool_conv: bfloat16 [16, 3, 8192], P(('groups', 'replica'), None, 'channel'), parts along dimension 0, may hold values from -6 to 6
- owner_id: int32 [2], P('groups'), parts along dimension 0, may hold values from 0 to 7
- readers: int32 [16], P(('groups', 'replica')), parts along dimension 0, may hold values 0 or 1
- restore_src: int32 [16, 4], P('groups'), parts along dimension 0, may hold values from 0 to 7, as said below
- restore_blk: int32 [16, 4], P('groups'), parts along dimension 0, may hold values from 0 to 3, as said below
- state_src: int32 [16], P('groups'), parts along dimension 0, may hold values from 0 to 7, as said below
- ctx_blocks: int32 [16], P(('groups', 'replica')), parts along dimension 0, may hold values from 1 to 4, as said below
- mamba_x: bfloat16 [16, 2, 32, 8192], P(('groups', 'replica'), None, None, 'channel'), parts along dimension 0, may hold values from -6 to 6
- mamba_z: bfloat16 [16, 2, 32, 8192], P(('groups', 'replica'), None, None, 'channel'), parts along dimension 0, may hold values from -6 to 6
- mamba_dt: bfloat16 [16, 2, 32, 8192], P(('groups', 'replica'), None, None, 'channel'), parts along dimension 0, may hold values from -2 to 8
- dt_bias: float32 [8192], P('channel'), may hold values from -6 to -2.5
- a_log: float32 [16, 8192], P(None, 'channel'), may hold values from 0 to 2
- bypass_gain: float32 [8192], P('channel'), may hold values from 0.5 to 1.5
- conv_w: float32 [4, 8192], P(None, 'channel'), may hold values from -3 to 3
- conv_b: float32 [8192], P('channel'), may hold values from -0.5 to 0.5
- w_bc: bfloat16 [8192, 32], P('channel'), may hold values from -0.0625 to 0.0625
Outputs:
- attention_out: bfloat16 [16, 2, 32, 4096], P(('groups', 'replica'), None, None, 'channel'), parts along dimension 0
- mamba_out: bfloat16 [16, 2, 32, 8192], P(('groups', 'replica'), None, None, 'channel'), parts along dimension 0
There are 2 independent parts, one for each index of `groups`. A program takes and returns all parts, laid end to end along the dimension named above; an argument that names none is the same for every part. Nothing has to cross between parts.
Inputs may be any that keep to these rules, and one draw needn't show every extreme that they name: `restore_src`: each row names 4 different replicas, and each replica is named in exactly 4 rows, so at most one block goes from one replica to one row's replica. Every pair (restore_src, restore_blk) is different: each stored block of each replica is listed exactly once. `state_src`: A permutation of the replicas. Only slots j < ctx_blocks[d] of row d are read; some replica has 4.
All inputs are finite; a program needn't handle non-finite values. No bound on the sum of `readers` on one device may be relied on, other than what follows from the above.
Results may differ from a plain program's by a relative error of at most 0.0049.
Values may be sent and summed in bfloat16 or wider, within the bound.
A program may use at most 128 MiB of HBM per device.

v0:
```python
import jax
import jax.numpy as jnp
from jax import lax
from jax.experimental import pallas as pl
from jax.experimental.pallas import tpu as pltpu
from jax.sharding import PartitionSpec as P

HD = 128
Q_PER_KV = 8
CHUNKS = 4


def attend_kernel(parts, src_ref, live_ref, q_ref, *refs):
    ctx_refs, new_ref, out_ref = refs[:parts], refs[parts], refs[parts + 1]
    new_len = q_ref.shape[0]
    heads = new_ref.shape[1] // (2 * HD)
    factor = HD ** (-0.5)
    rows = Q_PER_KV * new_len
    live = live_ref[0]
    for head in range(heads):
        query = jnp.concatenate(
            [
                q_ref[:, (head * Q_PER_KV + g) * HD : (head * Q_PER_KV + g + 1) * HD]
                for g in range(Q_PER_KV)
            ],
            axis=0,
        )
        key_cols = slice(2 * head * HD, (2 * head + 1) * HD)
        value_cols = slice((2 * head + 1) * HD, (2 * head + 2) * HD)
        contract = (((1,), (1,)), ((), ()))
        scores = []
        start = 0
        for ref in ctx_refs:
            piece = (
                lax.dot_general(
                    query, ref[:, key_cols], contract, preferred_element_type=jnp.float32
                )
                * factor
            )
            position = start + lax.broadcasted_iota(jnp.int32, piece.shape, 1)
            scores.append(jnp.where(position < live, piece, -jnp.inf))
            start += ref.shape[0]
        fresh = (
            lax.dot_general(
                query, new_ref[:, key_cols], contract, preferred_element_type=jnp.float32
            )
            * factor
        )
        time = lax.rem(lax.broadcasted_iota(jnp.int32, fresh.shape, 0), new_len)
        fresh = jnp.where(
            time >= lax.broadcasted_iota(jnp.int32, fresh.shape, 1), fresh, -jnp.inf
        )
        highest = jnp.max(fresh, axis=1, keepdims=True)
        for piece in scores:
            highest = jnp.maximum(highest, jnp.max(piece, axis=1, keepdims=True))
        weight = jnp.exp(fresh - highest)
        total = jnp.sum(weight, axis=1, keepdims=True)
        mixed = jnp.dot(
            weight.astype(jnp.bfloat16),
            new_ref[:, value_cols],
            preferred_element_type=jnp.float32,
        )
        for piece, ref in zip(scores, ctx_refs):
            weight = jnp.exp(piece - highest)
            total = total + jnp.sum(weight, axis=1, keepdims=True)
            mixed = mixed + jnp.dot(
                weight.astype(jnp.bfloat16),
                ref[:, value_cols],
                preferred_element_type=jnp.float32,
            )
        result = (mixed / total).astype(out_ref.dtype)
        for g in range(Q_PER_KV):
            at = (head * Q_PER_KV + g) * HD
            out_ref[:, at : at + HD] = result[g * new_len : (g + 1) * new_len]


def attend(request, queries, blocks, block_len, source, live, new_kv):
    parts = source.shape[0]
    width = blocks.shape[1]
    _, _, new_len, q_width = queries.shape

    def pick(j):
        return pl.BlockSpec((block_len, width), lambda i, s, l: (s[j], 0))

    return pl.pallas_call(
        lambda *refs: attend_kernel(parts, *refs),
        grid_spec=pltpu.PrefetchScalarGridSpec(
            num_scalar_prefetch=2,
            grid=(1,),
            in_specs=[
                pl.BlockSpec((None, None, new_len, q_width), lambda i, s, l: (0, request, 0, 0))
            ]
            + [pick(j) for j in range(parts)]
            + [pl.BlockSpec((None, None, new_len, width), lambda i, s, l: (0, request, 0, 0))],
            out_specs=pl.BlockSpec((new_len, q_width), lambda i, s, l: (0, 0)),
        ),
        out_shape=jax.ShapeDtypeStruct((new_len, q_width), jnp.bfloat16),
        name="attend",
    )(source, live, queries, *([blocks] * parts), new_kv)


def signal_kernel(read_ref, x_ref, shared_ref, pool_ref, w_ref, b_ref, wbc_ref, sig_ref, bc_ref, pad):
    taps = w_ref.shape[0]
    new_len = x_ref.shape[1]
    reading = read_ref[0] > 0
    base = 8 - (taps - 1)
    start = wbc_ref.shape[1] // 2
    shared = shared_ref[...].astype(jnp.float32)[start : start + taps - 1]
    pad[0, base:8] = jnp.where(reading, shared, 0.0)
    pad[1, base:8] = pool_ref[...].astype(jnp.float32)[start : start + taps - 1]

    @pl.when(pl.program_id(0) == 0)
    def _():
        bc_ref[...] = jnp.zeros_like(bc_ref)

    for r in range(2):
        pad[r, 8 : 8 + new_len] = x_ref[r].astype(jnp.float32)
        total = b_ref[...] + w_ref[0:1] * pad[r, base : base + new_len]
        for k in range(1, taps):
            total = total + w_ref[k : k + 1] * pad[r, base + k : base + k + new_len]
        signal = total * jax.nn.sigmoid(total)
        sig_ref[r] = signal
        bc_ref[r] += jnp.dot(
            signal.astype(jnp.bfloat16), wbc_ref[...], preferred_element_type=jnp.float32
        )


def signal_call(reading, x, shared, offset, pool, w, b, wbc):
    _, _, new_len, channels = x.shape
    taps, cols = w.shape[0], wbc.shape[1]
    chunk = pool.shape[2]
    return pl.pallas_call(
        signal_kernel,
        grid_spec=pltpu.PrefetchScalarGridSpec(
            num_scalar_prefetch=1,
            grid=(channels // chunk,),
            in_specs=[
                pl.BlockSpec((None, 2, new_len, chunk), lambda i, s: (0, 0, 0, i)),
                pl.BlockSpec((None, shared.shape[1], chunk), lambda i, s: (offset + i, 0, 0)),
                pl.BlockSpec((None, pool.shape[1], chunk), lambda i, s: (i, 0, 0)),
                pl.BlockSpec((taps, chunk), lambda i, s: (0, i)),
                pl.BlockSpec((1, chunk), lambda i, s: (0, i)),
                pl.BlockSpec((chunk, cols), lambda i, s: (i, 0)),
            ],
            out_specs=[
                pl.BlockSpec((2, new_len, chunk), lambda i, s: (0, 0, i)),
                pl.BlockSpec((2, new_len, cols), lambda i, s: (0, 0, 0)),
            ],
            scratch_shapes=[pltpu.VMEM((2, 8 + new_len, chunk), jnp.float32)],
        ),
        out_shape=[
            jax.ShapeDtypeStruct((2, new_len, channels), jnp.float32),
            jax.ShapeDtypeStruct((2, new_len, cols), jnp.float32),
        ],
        cost_estimate=pl.CostEstimate(flops=6_000_000_000, bytes_accessed=20_000_000, transcendentals=0),
        name="signal",
    )(reading, x, shared, pool, w, b, wbc)


def scan_kernel(
    read_ref, bc_ref, sig_ref, dt_ref, z_ref, bias_ref, alog_ref, gain_ref, shared_ref, pool_ref,
    out_ref, spread, step_buf, push_buf, scan_buf
):
    states, chunk = alog_ref.shape
    new_len = sig_ref.shape[1]

    @pl.when(pl.program_id(0) == 0)
    def _():
        for r in range(2):
            columns = bc_ref[r].T
            for t in range(new_len):
                spread[r, t] = jnp.broadcast_to(columns[:, t : t + 1], spread.shape[2:])

    decay = -jnp.exp(alog_ref[...])
    hidden = []
    for r in range(2):
        x = dt_ref[r].astype(jnp.float32) + bias_ref[...]
        step = jnp.maximum(x, 0.0) + jnp.log1p(jnp.exp(-jnp.abs(x)))
        step_buf[r] = step
        push_buf[r] = step * sig_ref[r]
    hidden = (
        jnp.where(read_ref[0] > 0, shared_ref[...].astype(jnp.float32)[:states], 0.0),
        pool_ref[...].astype(jnp.float32)[:states],
    )
    tiles = chunk // HD
    for t in range(new_len):
        state = []
        for r in range(2):
            now = jnp.broadcast_to(step_buf[r, t : t + 1], (states, chunk))
            push = jnp.broadcast_to(push_buf[r, t : t + 1], (states, chunk))
            both = spread[r, t]
            gain = jnp.concatenate([both[:states]] * tiles, axis=1)
            read = jnp.concatenate([both[states:]] * tiles, axis=1)
            new = jnp.exp(now * decay) * hidden[r] + gain * push
            scan_buf[r, t : t + 1] = jnp.sum(read * new, axis=0, keepdims=True)
            state.append(new)
        hidden = tuple(state)
    for r in range(2):
        z = z_ref[r].astype(jnp.float32)
        full = scan_buf[r] + gain_ref[...] * sig_ref[r]
        out_ref[r] = (full * (z * jax.nn.sigmoid(z))).astype(out_ref.dtype)


def scan_call(reading, bc, signal, dt, z, bias, alog, gain, shared, offset, pool):
    _, new_len, channels = signal.shape
    states, cols = alog.shape[0], bc.shape[2]
    chunk = pool.shape[2]
    row = pl.BlockSpec((1, chunk), lambda i, s: (0, i))
    state = pl.BlockSpec((states, chunk), lambda i, s: (0, i))
    seq = pl.BlockSpec((None, 2, new_len, chunk), lambda i, s: (0, 0, 0, i))
    return pl.pallas_call(
        scan_kernel,
        grid_spec=pltpu.PrefetchScalarGridSpec(
            num_scalar_prefetch=1,
            grid=(channels // chunk,),
            in_specs=[
                pl.BlockSpec((2, new_len, cols), lambda i, s: (0, 0, 0)),
                pl.BlockSpec((2, new_len, chunk), lambda i, s: (0, 0, i)),
                seq,
                seq,
                row,
                state,
                row,
                pl.BlockSpec((None, shared.shape[1], chunk), lambda i, s: (offset + i, 0, 0)),
                pl.BlockSpec((None, pool.shape[1], chunk), lambda i, s: (i, 0, 0)),
            ],
            out_specs=pl.BlockSpec((None, 2, new_len, chunk), lambda i, s: (0, 0, 0, i)),
            scratch_shapes=[
                pltpu.VMEM((2, new_len, cols, HD), jnp.float32),
                pltpu.VMEM((2, new_len, chunk), jnp.float32),
                pltpu.VMEM((2, new_len, chunk), jnp.float32),
                pltpu.VMEM((2, new_len, chunk), jnp.float32),
            ],
        ),
        out_shape=jax.ShapeDtypeStruct((1, 2, new_len, channels), jnp.bfloat16),
        cost_estimate=pl.CostEstimate(flops=10_000_000_000, bytes_accessed=30_000_000, transcendentals=0),
        name="scan",
    )(reading, bc, signal, dt, z, bias, alog, gain, shared, pool)


def exchange_kernel(
    n, owner_ref, holder_ref, prefix_ref, state_ref, shared_ref, states_ref,
    state_cand, state_send, own, side, rightward, leftward, to_right, to_left, final,
    sends, recvs, chain_sends, chain_recvs, local_sems
):
    me = lax.axis_index("replica")
    chunks = prefix_ref.shape[1]
    line, half = me // 2, lax.rem(me, 2)
    length = n // 2
    last = length - 1
    partner = line * 2 + 1 - half
    owner = owner_ref[0]
    owner_line = owner // 2
    barrier = pltpu.get_barrier_semaphore()
    for s in range(1, n):
        pl.semaphore_signal(
            barrier, inc=1, device_id={"replica": lax.rem(me + s, n)}, device_id_type=pl.DeviceIdType.MESH
        )

    def remote(source, target, send_sem, recv_sem, peer):
        return pltpu.make_async_remote_copy(
            src_ref=source,
            dst_ref=target,
            send_sem=send_sem,
            recv_sem=recv_sem,
            device_id={"replica": peer},
            device_id_type=pl.DeviceIdType.MESH,
        )

    def spread(kind, s, source, target):
        return remote(
            source, target, sends.at[kind, s], recvs.at[kind, s], lax.rem(me + s, n)
        )

    def chain(kind, c, source, target, peer):
        return remote(source, target, chain_sends.at[kind, c], chain_recvs.at[kind, c], peer)

    own_prefix = pltpu.make_async_copy(prefix_ref.at[half], own, local_sems.at[0])
    own_state = pltpu.make_async_copy(state_ref.at[me], state_cand.at[me], local_sems.at[1])
    own_prefix.start()
    own_state.start()
    pl.semaphore_wait(barrier, n - 1)

    first_state, second_state, sideways = [], [], []
    for s in range(1, n):
        copy = spread(0, s, state_ref.at[lax.rem(me + s, n)], state_cand.at[me])
        copy.start()
        first_state.append(copy)
    for c in range(chunks):
        copy = chain(0, c, prefix_ref.at[1 - half, c], side.at[c], partner)
        copy.start()
        sideways.append(copy)

    own_state.wait()
    for copy in first_state:
        copy.wait()
    for d in range(n):
        state_send[d] = state_cand[holder_ref[d]]
    for s in range(1, n):
        copy = spread(2, s, state_send.at[lax.rem(me + s, n)], states_ref.at[me])
        copy.start()
        second_state.append(copy)
    mine_state = pltpu.make_async_copy(state_send.at[me], states_ref.at[me], local_sems.at[3])
    mine_state.start()
    own_prefix.wait()

    def right_copy(c):
        return chain(1, c, to_right.at[c], rightward.at[c], lax.rem(me + 2, n))

    def left_copy(c):
        return chain(2, c, to_left.at[c], leftward.at[c], lax.rem(me + n - 2, n))

    def final_copy(c):
        return chain(3, c, final.at[c], shared_ref.at[half, c], partner)

    def keep_copy(c):
        return pltpu.make_async_copy(final.at[c], shared_ref.at[half, c], local_sems.at[4 + c])

    def here(c):
        return jnp.where(owner == me, own[c], side[c])

    near, far = jnp.minimum(line, last - line), jnp.maximum(line, last - line)
    steps = chunks + length - 1
    for t in range(steps):
        c_near, c_right, c_left, c_far = t - near, t - line, t - (last - line), t - far

        @pl.when((c_near >= 0) & (c_near < chunks))
        def _():
            chain(0, c_near, side.at[c_near], side.at[c_near], partner).wait_recv()

        @pl.when((c_right >= 0) & (c_right < chunks))
        def _():
            @pl.when(line > 0)
            def _():
                right_copy(c_right).wait_recv()

            @pl.when(line < last)
            def _():
                to_right[c_right] = jnp.where(
                    owner_line == line, here(c_right), rightward[c_right]
                )
                right_copy(c_right).start()

        @pl.when((c_left >= 0) & (c_left < chunks))
        def _():
            @pl.when(line < last)
            def _():
                left_copy(c_left).wait_recv()

            @pl.when(line > 0)
            def _():
                to_left[c_left] = jnp.where(owner_line == line, here(c_left), leftward[c_left])
                left_copy(c_left).start()

        @pl.when((c_far >= 0) & (c_far < chunks))
        def _():
            final[c_far] = jnp.where(
                owner_line == line,
                here(c_far),
                jnp.where(owner_line < line, rightward[c_far], leftward[c_far]),
            )
            final_copy(c_far).start()
            keep_copy(c_far).start()

    mine_state.wait()
    for copy in sideways:
        copy.wait_send()
    for c in range(chunks):
        keep_copy(c).wait()
        final_copy(c).wait()

        @pl.when(line < last)
        def _():
            right_copy(c).wait_send()

        @pl.when(line > 0)
        def _():
            left_copy(c).wait_send()

    for copy in second_state:
        copy.wait()


def exchange(owner_id, state_src, prefix, states):
    n = states.shape[0]
    any_spec = pl.BlockSpec(memory_space=pl.ANY)
    smem = pl.BlockSpec(memory_space=pltpu.SMEM)
    piece = pltpu.VMEM(prefix.shape[1:], prefix.dtype)
    chunks = prefix.shape[1]
    return pl.pallas_call(
        lambda *refs: exchange_kernel(n, *refs),
        in_specs=[smem, smem, any_spec, any_spec],
        out_specs=[any_spec] * 2,
        out_shape=[
            jax.ShapeDtypeStruct(prefix.shape, prefix.dtype),
            jax.ShapeDtypeStruct(states.shape, states.dtype),
        ],
        scratch_shapes=[
            pltpu.VMEM(states.shape, states.dtype),
            pltpu.VMEM(states.shape, states.dtype),
        ]
        + [piece] * 7
        + [
            pltpu.SemaphoreType.DMA((3, n)),
            pltpu.SemaphoreType.DMA((3, n)),
            pltpu.SemaphoreType.DMA((4, chunks)),
            pltpu.SemaphoreType.DMA((4, chunks)),
            pltpu.SemaphoreType.DMA((4 + chunks,)),
        ],
        compiler_params=pltpu.CompilerParams(collective_id=0, has_side_effects=True),
        cost_estimate=pl.CostEstimate(flops=40_000_000_000, bytes_accessed=100_000_000, transcendentals=0),
        name="exchange",
    )(owner_id, state_src, prefix, states)


def pack_states(ssm, conv, unit, width):
    rows = ssm.shape[0] + conv.shape[0]
    joined = jnp.pad(jnp.concatenate([ssm, conv], axis=0), ((0, -rows % unit), (0, 0)))
    return jnp.swapaxes(joined.reshape(joined.shape[0], -1, width), 0, 1)


def local(
    queries,
    new_kv,
    cached_lookup_pairs,
    prefix_ssm,
    prefix_conv,
    pool_kv,
    pool_ssm,
    pool_conv,
    owner_id,
    readers,
    restore_src,
    restore_blk,
    state_src,
    ctx_blocks,
    mamba_x,
    mamba_z,
    mamba_dt,
    dt_bias,
    a_log,
    bypass_gain,
    conv_w,
    conv_b,
    w_bc,
):
    block_len = pool_kv.shape[2]
    own_index = lax.axis_index("replica")
    my_sources = lax.dynamic_index_in_dim(restore_src, own_index, 0, keepdims=False)
    picked = jnp.sum(jnp.where(restore_src == own_index, restore_blk, 0), axis=1)
    send_kv = jnp.take(pool_kv[0], picked, axis=0, mode="clip")
    n, width, channels = restore_src.shape[0], cached_lookup_pairs.shape[2], pool_ssm.shape[2]
    length = cached_lookup_pairs.shape[1]
    pool_states = pack_states(pool_ssm[0], pool_conv[0], 8, channels // n)
    prefix_states = pack_states(prefix_ssm[0], prefix_conv[0], 16, width)
    groups, height = prefix_states.shape[:2]
    packed = jnp.concatenate([cached_lookup_pairs[0], prefix_states.reshape(-1, width)], axis=0)
    shared, pool_states = exchange(
        owner_id, state_src, packed.reshape(2, CHUNKS, -1, width), pool_states
    )
    send_kv, shared, pool_states = lax.optimization_barrier((send_kv, shared, pool_states))
    got_kv = lax.all_to_all(
        send_kv[:, None], "replica", split_axis=0, concat_axis=1, tiled=True
    )[0]
    shared = shared.reshape(packed.shape)
    if groups == n:
        offset = length // height
        prefix_states = shared.reshape(-1, height, width)
    else:
        offset = 0
        prefix_states = shared[length:].reshape(groups, height, width)
        prefix_states = jnp.swapaxes(prefix_states, 0, 1).reshape(height, n, channels // n)
        prefix_states = jnp.swapaxes(prefix_states, 0, 1)
    reading = (readers > 0).astype(jnp.int32)
    signal, partial_bc = signal_call(
        reading, mamba_x, prefix_states, offset, pool_states, conv_w, conv_b[None], w_bc
    )
    state_bc = lax.psum(partial_bc, "channel")
    mamba_out = scan_call(
        reading, state_bc, signal, mamba_dt, mamba_z, dt_bias[None], a_log, bypass_gain[None],
        prefix_states, offset, pool_states
    )
    parts = length // block_len
    fresh_out = attend(
        0, queries, shared, block_len, lax.iota(jnp.int32, parts), reading * length, new_kv
    )
    got_kv, mamba_out, fresh_out = lax.optimization_barrier((got_kv, mamba_out, fresh_out))
    resumed_out = attend(
        1, queries, got_kv.reshape(-1, width), block_len, my_sources, ctx_blocks * block_len, new_kv
    )
    return (jnp.stack([fresh_out, resumed_out])[None], mamba_out)


def placed_specs():
    return (
        P(("groups", "replica"), None, None, "channel"),
        P(("groups", "replica"), None, None, "channel"),
        P(("groups", "replica"), None, "channel"),
        P(("groups", "replica"), None, "channel"),
        P(("groups", "replica"), None, "channel"),
        P(("groups", "replica"), None, None, "channel"),
        P(("groups", "replica"), None, "channel"),
        P(("groups", "replica"), None, "channel"),
        P("groups"),
        P(("groups", "replica")),
        P("groups", None),
        P("groups", None),
        P("groups"),
        P(("groups", "replica")),
        P(("groups", "replica"), None, None, "channel"),
        P(("groups", "replica"), None, None, "channel"),
        P(("groups", "replica"), None, None, "channel"),
        P("channel"),
        P(None, "channel"),
        P("channel"),
        P(None, "channel"),
        P("channel"),
        P("channel", None),
    )


def solution(mesh):
    return jax.shard_map(
        local,
        mesh=mesh,
        in_specs=placed_specs(),
        out_specs=(
            P(("groups", "replica"), None, None, "channel"),
            P(("groups", "replica"), None, None, "channel"),
        ),
        check_vma=False,
    )
```

profile of v0, /device:TPU:0, one launch (start us, length us, event | category | flops | bytes accessed | tf_op | source)
XLA Modules:
  0.0 113.5 jit_solution(2775741532891002294)
XLA Ops:
  0.6 0.0 copy-start
  0.6 0.8 select_reduce_fusion
  1.5 1.0 fusion.4
  2.4 0.1 copy.34
  2.5 0.1 copy.30
  2.6 1.0 fusion.5
  3.6 0.7 copy.36
  4.9 0.0 copy-done
  4.9 0.0 copy-start.2
  4.9 2.0 %gather_fusion = bf16[8,256,512]{2,1,0:T(8,128)(2,1)} fusion(bf16[4,256,512]{2,1,0:T(8,128)(2,1)S(1)} %bitcast.31, s32[1024]{0:T(1024)S(1)} %pad_clamp_fusion), kind=kCustom, calls=%fused_computation | custom fusion | bytes 4194336 | tf_op jit(solution)/shard_map/jit(_take)/gather | solution.py:451
  6.9 0.0 copy-done.2
  6.9 1.2 %pad_maximum_fusion = bf16[1280,512]{1,0:T(8,128)(2,1)} fusion(bf16[256,512]{1,0:T(8,128)(2,1)S(1)} %bitcast.44, bf16[1024,512]{1,0:T(8,128)(2,1)S(1)} %bitcast.45), kind=kLoop, calls=%fused_computation.1 | loop fusion | flops 2621440 | bytes 2621440 | tf_op jit(solution)/shard_map/concatenate | solution.py:457
  8.1 48.6 %exchange.1 = (bf16[2,4,160,512]{3,2,1,0:T(8,128)(2,1)}, bf16[8,24,512]{2,1,0:T(8,128)(2,1)}) custom-call(s32[1]{0:T(128)S(6)} %copy.37.refs_0_, s32[8]{0:T(128)} %refs_1_.1, bf16[2,4,160,512]{3,2,1,0:T(8,128)(2,1)} %bitcast.43, bf16[8,24,512]{2,1,0:T(8,128)(2,1)} %bitcast.51), custom_call_target="tpu_custom_call" | custom-call | flops 40000000000 | bytes 100000000 | tf_op jit(solution)/shard_map/exchange/pallas_call | solution.py:390
  56.7 0.0 copy-start.4
  56.7 0.0 copy-start.5
  56.7 3.7 %all-to-all-start = ((bf16[8,1,256,512]{3,2,1,0:T(8,128)(2,1)}), bf16[8,1,256,512]{3,2,1,0:T(8,128)(2,1)S(1)}, u32[]{:S(2)}, u32[]{:S(2)}) async-start(bf16[8,1,256,512]{3,2,1,0:T(8,128)(2,1)} %bitcast.42), calls=%async_computation | async-start | bytes 4194304 | tf_op jit(solution)/shard_map/all_to_all | solution.py:462
  61.1 0.0 copy-done.4
  61.1 1.3 %copy.32.wbc_ref = bf16[4096,32]{1,0:T(8,128)(2,1)} copy(bf16[4096,32]{0,1:T(8,128)(2,1)S(1)} %copy-done.4) | data formatting | bytes 524288 | tf_op args[22]
  62.5 0.0 copy-done.5
  62.5 0.7 dynamic-slice_reduce_fusion.refs_0_
  63.8 0.5 iota.3.refs_0_
  64.3 3.8 %attend.2 = bf16[32,2048]{1,0:T(8,128)(2,1)} custom-call(s32[4]{0:T(128)} %iota.3.refs_0_, s32[1]{0:T(128)S(6)} %mul.6.refs_1_, bf16[1,2,32,2048]{3,2,1,0:T(8,128)(2,1)} %refs_2_.3, bf16[1280,512]{1,0:T(8,128)(2,1)} %bitcast.36, bf16[1280,512]{1,0:T(8,128)(2,1)} %bitcast.37, bf16[1280,512]{1,0:T(8,128)(2,1)} %bitcast.38, bf16[1280,512]{1,0:T(8,128)(2,1)} %bitcast.39, ...), custom_call_target="tpu_custom_call" | custom-call | tf_op jit(solution)/shard_map/attend/pallas_call | solution.py:85
  68.1 6.4 %signal.1 = (f32[2,32,4096]{2,1,0:T(8,128)}, f32[2,32,32]{2,1,0:T(8,128)}) custom-call(s32[1]{0:T(128)S(6)} %convert_element_type.7.read_ref, bf16[1,2,32,4096]{3,2,1,0:T(8,128)(2,1)} %x_ref.1, bf16[40,32,512]{2,1,0:T(8,128)(2,1)} %bitcast.40, bf16[8,24,512]{2,1,0:T(8,128)(2,1)} %get-tuple-element.16.pool_ref, f32[4,4096]{1,0:T(4,128)} %w_ref.1, ...), custom_call_target="tpu_custom_call" | custom-call | flops 6000000000 | bytes 20000000 | tf_op jit(solution)/shard_map/signal/pallas_call | solution.py:132
  74.5 4.6 %psum.7.bc_ref = f32[2,32,32]{2,1,0:T(8,128)} all-reduce(f32[2,32,32]{2,1,0:T(8,128)} %get-tuple-element.17), channel_id=1, replica_groups=mesh['groups'=2,'replica'=8,'channel'=2] {'channel'}, use_global_device_ids=true, to_apply=%region_1.2 | all-reduce | flops 2048 | bytes 16384 | tf_op jit(solution)/shard_map/psum | solution.py:478
  79.1 9.8 %scan.1 = bf16[1,2,32,4096]{3,2,1,0:T(8,128)(2,1)} custom-call(s32[1]{0:T(128)S(6)} %convert_element_type.7.read_ref, f32[2,32,32]{2,1,0:T(8,128)} %psum.7.bc_ref, f32[2,32,4096]{2,1,0:T(8,128)} %get-tuple-element.18.sig_ref, bf16[1,2,32,4096]{3,2,1,0:T(8,128)(2,1)} %dt_ref.1, bf16[1,2,32,4096]{3,2,1,0:T(8,128)(2,1)} %z_ref.1, f32[1,4096]{1,0:T(1,128)} %bitcast.57, ...), custom_call_target="tpu_custom_call" | custom-call | flops 10000000000 | bytes 30000000 | tf_op jit(solution)/shard_map/scan/pallas_call | solution.py:211
  88.9 17.7 %all-to-all-done = bf16[8,1,256,512]{3,2,1,0:T(8,128)(2,1)S(1)} async-done(((bf16[8,1,256,512]{3,2,1,0:T(8,128)(2,1)}), bf16[8,1,256,512]{3,2,1,0:T(8,128)(2,1)S(1)}, u32[]{:S(2)}, u32[]{:S(2)}) %all-to-all-start) | async-done | bytes 2097184 | tf_op jit(solution)/shard_map/all_to_all | solution.py:462
  106.6 0.0 copy-start.1
  106.6 1.3 %copy-done.1 = bf16[8,1,256,512]{3,2,1,0:T(8,128)(2,1)} copy-done((bf16[8,1,256,512]{3,2,1,0:T(8,128)(2,1)}, bf16[8,1,256,512]{3,2,1,0:T(8,128)(2,1)S(1)}, u32[]{:S(2)}) %copy-start.1) | copy-done | bytes 2097176
  108.0 0.0 copy-start.3
  108.0 3.9 %attend.3 = bf16[32,2048]{1,0:T(8,128)(2,1)} custom-call(s32[4]{0:T(128)} %dynamic-slice_reduce_fusion.refs_0_, s32[1]{0:T(128)S(6)} %mul.7.refs_1_, bf16[1,2,32,2048]{3,2,1,0:T(8,128)(2,1)} %refs_2_.3, bf16[2048,512]{1,0:T(8,128)(2,1)} %bitcast.32, bf16[2048,512]{1,0:T(8,128)(2,1)} %bitcast.33, bf16[2048,512]{1,0:T(8,128)(2,1)} %bitcast.34, ...), custom_call_target="tpu_custom_call" | custom-call | tf_op jit(solution)/shard_map/attend/pallas_call | solution.py:85
  111.9 0.0 copy-done.3
  111.9 1.6 %maximum_bitcast_fusion = bf16[1,2,32,2048]{3,2,1,0:T(8,128)(2,1)} fusion(bf16[1,32,2048]{2,1,0:T(8,128)(2,1)} %bitcast.49, bf16[1,32,2048]{2,1,0:T(8,128)(2,1)S(1)} %bitcast.50), kind=kLoop, calls=%fused_computation.9 | loop fusion | flops 131072 | bytes 524288 | tf_op jit(solution)/shard_map/broadcast_in_dim | solution.py:491
  (1 shorter events, 0.0 us)
Async XLA Ops:
  0.6 4.3 %copy-start = (bf16[1,4,256,512]{3,2,1,0:T(8,128)(2,1)S(1)}, bf16[1,4,256,512]{3,2,1,0:T(8,128)(2,1)}, u32[]{:S(2)}) copy-start(bf16[1,4,256,512]{3,2,1,0:T(8,128)(2,1)} %param.28) | copy-start | bytes 3145732
  4.9 2.0 %copy-start.2 = (bf16[1,1024,512]{2,1,0:T(8,128)(2,1)S(1)}, bf16[1,1024,512]{2,1,0:T(8,128)(2,1)}, u32[]{:S(2)}) copy-start(bf16[1,1024,512]{2,1,0:T(8,128)(2,1)} %param.25) | copy-start | bytes 3145732
  56.7 4.4 %copy-start.4 = (bf16[4096,32]{0,1:T(8,128)(2,1)S(1)}, bf16[4096,32]{0,1:T(8,128)(2,1)}, u32[]{:S(2)}) copy-start(bf16[4096,32]{0,1:T(8,128)(2,1)} %param.45) | copy-start | bytes 786436
  56.7 5.8 %copy-start.5 = (s32[8,4]{0,1:T(4,128)S(1)}, s32[8,4]{0,1:T(4,128)}, u32[]{:S(2)}) copy-start(s32[8,4]{0,1:T(4,128)} %param.33) | copy-start | bytes 388
  56.7 49.9 %all-to-all-start = ((bf16[8,1,256,512]{3,2,1,0:T(8,128)(2,1)}), bf16[8,1,256,512]{3,2,1,0:T(8,128)(2,1)S(1)}, u32[]{:S(2)}, u32[]{:S(2)}) async-start(bf16[8,1,256,512]{3,2,1,0:T(8,128)(2,1)} %bitcast.42), calls=%async_computation | async-start | bytes 4194304 | tf_op jit(solution)/shard_map/all_to_all | solution.py:462
  106.6 1.3 %copy-start.1 = (bf16[8,1,256,512]{3,2,1,0:T(8,128)(2,1)}, bf16[8,1,256,512]{3,2,1,0:T(8,128)(2,1)S(1)}, u32[]{:S(2)}) copy-start(bf16[8,1,256,512]{3,2,1,0:T(8,128)(2,1)S(1)} %all-to-all-done) | copy-start | bytes 6291460
  108.0 3.9 %copy-start.3 = (bf16[32,2048]{1,0:T(8,128)(2,1)S(1)}, bf16[32,2048]{1,0:T(8,128)(2,1)}, u32[]{:S(2)}) copy-start(bf16[32,2048]{1,0:T(8,128)(2,1)} %attend.2) | copy-start | bytes 393220
where the time goes:
time: 114 us
  Pallas kernels  72.5 us (64%)
  waiting for transfers between devices  17.7 us (16%)
  local copies, waits for them, and re-layouts  6.79 us (6%)
  other arithmetic  5.5 us (5%)
  blocking collectives  4.63 us (4%)
  starting transfers between devices  3.75 us (3%)
  between operations  2.68 us (2%)
    pallas_call x1, Pallas kernels, exchange(): pl.pallas_call(lambda *refs: exchange_kernel(n, *refs), in_specs=[smem, s...  48.6 us
    all_to_all x1, waiting for transfers between devices, local(): lax.all_to_all(send_kv[:, None], 'replica', split_axis=0, concat_axis=1,...  17.7 us
    pallas_call x1, Pallas kernels, scan_call(): pl.pallas_call(scan_kernel, grid_spec=pltpu.PrefetchScalarGridSpec(num_sc...  9.8 us
    pallas_call x2, Pallas kernels, attend(): pl.pallas_call(lambda *refs: attend_kernel(parts, *refs), grid_spec=pltpu...  7.73 us
    pallas_call x1, Pallas kernels, signal_call(): pl.pallas_call(signal_kernel, grid_spec=pltpu.PrefetchScalarGridSpec(num_...  6.38 us
    psum x1, blocking collectives, local(): state_bc = lax.psum(partial_bc, 'channel')  4.63 us
    all_to_all x1, starting transfers between devices, local(): lax.all_to_all(send_kv[:, None], 'replica', split_axis=0, concat_axis=1,...  3.75 us
    unnamed x14, local copies, waits for them, and re-layouts  2.78 us
  transfers between devices with their start and end apart: 1, of which 1 were waited for; matrix products, arithmetic and copies ran while one was open for 2% of the time, Pallas kernels for 18%

commit v1 on v0

v1 whole, which is shorter than its diff:
```python
import jax
import jax.numpy as jnp
from jax import lax
from jax.experimental import pallas as pl
from jax.experimental.pallas import tpu as pltpu
from jax.sharding import PartitionSpec as P

HD = 128
Q_PER_KV = 8
KV_CHUNKS = 8
MESH = pl.DeviceIdType.MESH


def scores_of(keys, query):
    contract = (((1,), (1,)), ((), ()))
    return lax.dot_general(keys, query, contract, preferred_element_type=jnp.float32) * (HD ** (-0.5))


def mix(values, weight):
    contract = (((0,), (0,)), ((), ()))
    return lax.dot_general(values, weight.astype(jnp.bfloat16), contract, preferred_element_type=jnp.float32)


def layer_kernel(
    n,
    owner_ref, read_ref, src_ref, blk_ref, holder_ref, ctx_ref,
    q_ref, new_ref, kv_ref, pssm_ref, pool_ref, ossm_ref, conv_ref,
    x_ref, z_ref, dt_ref, bias_ref, alog_ref, gain_ref, cw_ref, cb_ref, wbc_ref,
    att_ref, mam_ref,
    q_all, pool_v, part_o, part_s, got_o, got_s,
    cand, piece, states,
    own, side, rightward, leftward, to_right, to_left, shared,
    q0_v, new_v, x_v, z_v, dt_v, bias_v, alog_v, gain_v, cw_v, cb_v, wbc_v,
    pad, sig, bc_mine, bc_theirs, spread, step_buf, push_buf, scan_buf,
    load_sems, own_sems, st_send, st_recv, p_send, p_recv, q_send, q_recv,
    ch_send, ch_recv, bc_send, bc_recv,
):
    me = lax.axis_index("replica")
    core = lax.axis_index("channel")
    line, half = me // 2, lax.rem(me, 2)
    length = n // 2
    last = length - 1
    partner = line * 2 + 1 - half
    owner = owner_ref[0]
    owner_line = owner // 2
    reading = read_ref[0] > 0
    states_n, channels = alog_v.shape
    new_len = q0_v.shape[0]
    heads = new_v.shape[2] // (2 * HD)
    rows = Q_PER_KV * new_len
    chunks, _, width = side.shape
    piece_w = cand.shape[2]
    per = width // piece_w
    wide = channels // width
    blocks_listed = src_ref.shape[0]

    barrier = pltpu.get_barrier_semaphore()
    for s in range(1, n):
        pl.semaphore_signal(
            barrier, inc=1, device_id={"replica": lax.rem(me + s, n)}, device_id_type=MESH
        )
    pl.semaphore_signal(barrier, inc=1, device_id={"channel": 1 - core}, device_id_type=MESH)

    loads = []

    def load(source, target):
        copy = pltpu.make_async_copy(source, target, load_sems.at[len(loads)])
        copy.start()
        loads.append(copy)
        return copy

    load_q = load(q_ref.at[0, 1], q_all.at[me])
    load_kv = load(kv_ref, own.at[:, pl.ds(1, chunks - 1)])
    load_ssm = []
    per_half = wide // 2
    for g in range(wide):
        load_ssm.append(
            load(
                pssm_ref.at[0, :, pl.ds(g * width, width)],
                own.at[g // per_half, 0, pl.ds(g % per_half * states_n, states_n)],
            )
        )
    mine = pl.ds(pl.multiple_of(me * piece_w, piece_w), piece_w)
    load_cand = [
        load(ossm_ref.at[0, :, mine], cand.at[me, pl.ds(0, states_n)]),
        load(conv_ref.at[:, mine], cand.at[me, pl.ds(states_n, 8)]),
    ]
    load_pool = load(pool_ref.at[0], pool_v)
    load_conv = [load(x_ref.at[0], x_v), load(cw_ref, cw_v), load(cb_ref, cb_v), load(wbc_ref, wbc_v)]
    load_scan = [
        load(dt_ref.at[0], dt_v), load(z_ref.at[0], z_v), load(bias_ref, bias_v),
        load(alog_ref, alog_v), load(gain_ref, gain_v),
    ]
    load_att = [load(q_ref.at[0, 0], q0_v), load(new_ref.at[0], new_v)]

    def remote(source, target, send_sem, recv_sem, peer):
        return pltpu.make_async_remote_copy(
            src_ref=source, dst_ref=target, send_sem=send_sem, recv_sem=recv_sem,
            device_id={"replica": peer}, device_id_type=MESH,
        )

    def peer_of(s):
        return lax.rem(me + s, n)

    load_q.wait()
    pl.semaphore_wait(barrier, n)

    def q_right(s):
        item = q_all.at[(line - s) * 2 + half]
        return remote(item, item, q_send.at[0, s], q_recv.at[0, s], lax.rem(me + 2, n))

    def q_left(s):
        item = q_all.at[(line + s) * 2 + half]
        return remote(item, item, q_send.at[1, s], q_recv.at[1, s], lax.rem(me + n - 2, n))

    def q_from_left(s):
        item = q_all.at[(line - s) * 2 + half]
        return remote(item, item, q_send.at[0, s - 1], q_recv.at[0, s - 1], partner)

    def q_from_right(s):
        item = q_all.at[(line + s) * 2 + half]
        return remote(item, item, q_send.at[1, s - 1], q_recv.at[1, s - 1], partner)

    def q_over(s):
        item = q_all.at[(line + s) * 2 + half]
        index = length - 1 + s
        return remote(item, item, q_send.at[2, index], q_recv.at[2, index], partner)

    @pl.when(line < last)
    def _():
        q_right(0).start()

    @pl.when(line > 0)
    def _():
        q_left(0).start()

    q_over(0).start()

    def state_first(kind, s):
        peer = peer_of(s)
        cols = pl.ds(pl.multiple_of(peer * piece_w, piece_w), piece_w)
        if kind == 0:
            source, target = ossm_ref.at[0, :, cols], cand.at[me, pl.ds(0, states_n)]
        else:
            source, target = conv_ref.at[:, cols], cand.at[me, pl.ds(states_n, 8)]
        return remote(source, target, st_send.at[kind, s], st_recv.at[kind, s], peer)

    def state_second(s):
        peer = peer_of(s)
        return remote(piece.at[peer], states.at[me], st_send.at[2, s], st_recv.at[2, s], peer)

    for s in range(1, n):
        state_first(0, s).start()
        state_first(1, s).start()

    def chain(kind, c, source, target, peer):
        return remote(source, target, ch_send.at[kind, c], ch_recv.at[kind, c], peer)

    def side_copy(c):
        return chain(0, c, own.at[1 - half, c], side.at[c], partner)

    def right_copy(c):
        return chain(1, c, to_right.at[c], rightward.at[c], lax.rem(me + 2, n))

    def left_copy(c):
        return chain(2, c, to_left.at[c], leftward.at[c], lax.rem(me + n - 2, n))

    def final_copy(c):
        return chain(3, c, shared.at[half, c], shared.at[half, c], partner)

    def here(c):
        return jnp.where(owner == me, own[half, c], side[c])

    near, far = jnp.minimum(line, last - line), jnp.maximum(line, last - line)

    def spread_step(t):
        if t + 1 < chunks:
            side_copy(t + 1).start()
        c_near, c_right, c_left, c_far = t - near, t - line, t - (last - line), t - far

        @pl.when((c_near >= 0) & (c_near < chunks))
        def _():
            side_copy(c_near).wait_recv()

        @pl.when((c_right >= 0) & (c_right < chunks))
        def _():
            @pl.when(line > 0)
            def _():
                right_copy(c_right).wait_recv()

            @pl.when(line < last)
            def _():
                to_right[c_right] = jnp.where(owner_line == line, here(c_right), rightward[c_right])
                right_copy(c_right).start()

        @pl.when((c_left >= 0) & (c_left < chunks))
        def _():
            @pl.when(line < last)
            def _():
                left_copy(c_left).wait_recv()

            @pl.when(line > 0)
            def _():
                to_left[c_left] = jnp.where(owner_line == line, here(c_left), leftward[c_left])
                left_copy(c_left).start()

        @pl.when((c_far >= 0) & (c_far < chunks))
        def _():
            shared[half, c_far] = jnp.where(
                owner_line == line,
                here(c_far),
                jnp.where(owner_line < line, rightward[c_far], leftward[c_far]),
            )
            final_copy(c_far).start()

    load_kv.wait()
    for copy in load_ssm:
        copy.wait()
    side_copy(0).start()

    for copy in load_cand:
        copy.wait()
    for s in range(1, n):
        state_first(0, s).wait_recv()
        state_first(1, s).wait_recv()
    conv_row = lax.broadcasted_iota(jnp.int32, (8, piece_w), 0)
    shared_conv = cand[owner, states_n:].astype(jnp.float32)
    for d in range(n):
        holder = holder_ref[d]
        piece[d, :states_n] = cand[holder, :states_n]
        stored_conv = cand[holder, states_n:].astype(jnp.float32)
        piece[d, states_n:] = jnp.where(conv_row < 3, stored_conv, shared_conv).astype(piece.dtype)
    for s in range(1, n):
        state_second(s).start()
    states[me] = piece[me]

    def query_rows(load_piece, head):
        return jnp.concatenate(
            [load_piece((head * Q_PER_KV + g) * HD) for g in range(Q_PER_KV)], axis=0
        )

    def key_cols(head):
        return slice(2 * head * HD, (2 * head + 1) * HD)

    def value_cols(head):
        return slice((2 * head + 1) * HD, (2 * head + 2) * HD)

    def partial(d, out_o, out_s):
        block = jnp.int32(0)
        for j in range(blocks_listed):
            block = block + jnp.where(src_ref[j, d] == me, blk_ref[j, d], 0)
        for head in range(heads):
            query = query_rows(lambda at: q_all[d, :, at : at + HD], head)
            score = scores_of(pool_v[block, :, key_cols(head)], query)
            highest = jnp.max(score, axis=0, keepdims=True)
            weight = jnp.exp(score - highest)
            mixed = mix(pool_v[block, :, value_cols(head)], weight)
            out_o[head * HD : (head + 1) * HD] = mixed.astype(jnp.bfloat16)
            out_s[head : head + 1] = highest
            out_s[heads + head : heads + head + 1] = jnp.sum(weight, axis=0, keepdims=True)

    def part_copies(s):
        peer = peer_of(s)
        return (
            remote(part_o.at[peer], got_o.at[me], p_send.at[0, s], p_recv.at[0, s], peer),
            remote(part_s.at[peer], got_s.at[me], p_send.at[1, s], p_recv.at[1, s], peer),
        )

    def relay_unit(s):
        def go():
            @pl.when(line - s >= 0)
            def _():
                q_from_left(s).wait_recv()

                @pl.when(line < last)
                def _():
                    q_right(s).start()

                q_over(-s).start()

            @pl.when(line + s <= last)
            def _():
                q_from_right(s).wait_recv()

                @pl.when(line > 0)
                def _():
                    q_left(s).start()

                q_over(s).start()

        return go

    def gathered():
        for s in range(-last, length):
            @pl.when((line + s >= 0) & (line + s <= last))
            def _():
                q_over(s).wait_recv()

        load_pool.wait()

    def visit_unit(low, high):
        def go():
            if low == 1:
                gathered()
                partial(me, got_o.at[me], got_s.at[me])

            def body(s, carry):
                peer = peer_of(s)
                partial(peer, part_o.at[peer], part_s.at[peer])
                for copy in part_copies(s):
                    copy.start()
                return carry

            lax.fori_loop(low, high, body, 0)

        return go

    taps = cw_v.shape[0]
    base = 8 - (taps - 1)

    def lanes(i):
        return pl.ds(pl.multiple_of(i * width, width), width)

    def stored(i):
        parts = [states[i * per + k].astype(jnp.float32) for k in range(per)]
        return parts[0] if per == 1 else jnp.concatenate(parts, axis=1)

    def bc_copy():
        return pltpu.make_async_remote_copy(
            src_ref=bc_mine, dst_ref=bc_theirs, send_sem=bc_send.at[0], recv_sem=bc_recv.at[0],
            device_id={"channel": 1 - core}, device_id_type=MESH,
        )

    def signal_unit(low, high):
        def go():
            if low == 0:
                for s in range(1, n):
                    state_second(s).wait_recv()
                for copy in load_conv:
                    copy.wait()
                bc_mine[...] = jnp.zeros_like(bc_mine)

            def body(i, carry):
                held = stored(i)[states_n:]
                pad[0, base:8] = jnp.where(reading, held[taps - 1 : 2 * taps - 2], 0.0)
                pad[1, base:8] = held[: taps - 1]
                both = []
                for r in range(2):
                    pad[r, 8 : 8 + new_len] = x_v[r, :, lanes(i)].astype(jnp.float32)
                    total = cb_v[:, lanes(i)] + cw_v[0:1, lanes(i)] * pad[r, base : base + new_len]
                    for k in range(1, taps):
                        total = total + cw_v[k : k + 1, lanes(i)] * pad[r, base + k : base + k + new_len]
                    signal = total * jax.nn.sigmoid(total)
                    sig[r, :, lanes(i)] = signal
                    both.append(signal.astype(jnp.bfloat16))
                bc_mine[:, : 2 * new_len] += lax.dot_general(
                    wbc_v[:, lanes(i)], jnp.concatenate(both, axis=0), (((1,), (1,)), ((), ())),
                    preferred_element_type=jnp.float32,
                )
                return carry

            lax.fori_loop(low, high, body, 0)
            if high == wide:
                bc_copy().start()

        return go

    def scan_unit(low, high):
        def go():
            if low == 0:
                bc_copy().wait_recv()
                total = bc_mine[...] + bc_theirs[...]
                for r in range(2):
                    for t in range(new_len):
                        at = r * new_len + t
                        spread[r, t] = jnp.broadcast_to(total[:, at : at + 1], spread.shape[2:])
                for copy in load_scan:
                    copy.wait()
                final_copy(0).wait_recv()

            def body(i, carry):
                decay = -jnp.exp(alog_v[:, lanes(i)])
                for r in range(2):
                    x = dt_v[r, :, lanes(i)].astype(jnp.float32) + bias_v[:, lanes(i)]
                    step = jnp.maximum(x, 0.0) + jnp.log1p(jnp.exp(-jnp.abs(x)))
                    step_buf[r] = step
                    push_buf[r] = step * sig[r, :, lanes(i)]
                group = pl.ds(pl.multiple_of(lax.rem(i, per_half) * states_n, states_n), states_n)
                first = shared[i // per_half, 0, group].astype(jnp.float32)
                hidden = [jnp.where(reading, first, 0.0), stored(i)[:states_n]]
                tiles = width // HD
                for t in range(new_len):
                    for r in range(2):
                        now = jnp.broadcast_to(step_buf[r, t : t + 1], (states_n, width))
                        push = jnp.broadcast_to(push_buf[r, t : t + 1], (states_n, width))
                        both = spread[r, t]
                        gain = jnp.concatenate([both[:states_n]] * tiles, axis=1)
                        read = jnp.concatenate([both[states_n:]] * tiles, axis=1)
                        hidden[r] = jnp.exp(now * decay) * hidden[r] + gain * push
                        scan_buf[r, t : t + 1] = jnp.sum(read * hidden[r], axis=0, keepdims=True)
                for r in range(2):
                    z = z_v[r, :, lanes(i)].astype(jnp.float32)
                    full = scan_buf[r] + gain_v[:, lanes(i)] * sig[r, :, lanes(i)]
                    mam_ref[0, r, :, lanes(i)] = (full * (z * jax.nn.sigmoid(z))).astype(mam_ref.dtype)
                return carry

            lax.fori_loop(low, high, body, 0)

        return go

    visits = [1 + (n - 1) * k // 2 for k in range(3)]
    units = [relay_unit(s) for s in range(1, length)]
    units += [visit_unit(low, high) for low, high in zip(visits[:-1], visits[1:])]
    units += [signal_unit(0, wide // 2), signal_unit(wide // 2, wide)]
    units += [scan_unit(k * wide // 4, (k + 1) * wide // 4) for k in range(4)]
    steps = chunks + length - 1
    done = 0
    for t in range(steps):
        spread_step(t)
        until = (t + 1) * len(units) // steps
        for unit in units[done:until]:
            unit()
        done = until

    for c in range(1, chunks):
        final_copy(c).wait_recv()
    for copy in load_att:
        copy.wait()

    def causal(score):
        key = lax.broadcasted_iota(jnp.int32, score.shape, 0)
        time = lax.rem(lax.broadcasted_iota(jnp.int32, score.shape, 1), new_len)
        return jnp.where(time >= key, score, -jnp.inf)

    def put(request, head, mixed, total):
        result = (mixed / total).T.astype(att_ref.dtype)
        for g in range(Q_PER_KV):
            at = (head * Q_PER_KV + g) * HD
            att_ref[0, request, :, at : at + HD] = result[g * new_len : (g + 1) * new_len]

    for head in range(heads):
        query = query_rows(lambda at: q0_v[:, at : at + HD], head)
        fresh = causal(scores_of(new_v[0, :, key_cols(head)], query))
        highest = jnp.max(fresh, axis=0, keepdims=True)
        scores = []
        for h in range(2):
            keys = shared[h, 1:, :, key_cols(head)].reshape(-1, HD)
            score = jnp.where(reading, scores_of(keys, query), -jnp.inf)
            highest = jnp.maximum(highest, jnp.max(score, axis=0, keepdims=True))
            scores.append(score)
        weight = jnp.exp(fresh - highest)
        total = jnp.sum(weight, axis=0, keepdims=True)
        mixed = mix(new_v[0, :, value_cols(head)], weight)
        for h in range(2):
            weight = jnp.exp(scores[h] - highest)
            total = total + jnp.sum(weight, axis=0, keepdims=True)
            mixed = mixed + mix(shared[h, 1:, :, value_cols(head)].reshape(-1, HD), weight)
        put(0, head, mixed, total)

    for s in range(1, n):
        for copy in part_copies(s):
            copy.wait_recv()
    live = ctx_ref[0]
    for head in range(heads):
        query = query_rows(lambda at: q_all[me, :, at : at + HD], head)
        fresh = causal(scores_of(new_v[1, :, key_cols(head)], query))
        highest = jnp.max(fresh, axis=0, keepdims=True)
        tops = []
        for j in range(blocks_listed):
            top = jnp.where(j < live, got_s[src_ref[j, me], head : head + 1], -jnp.inf)
            tops.append(top)
            highest = jnp.maximum(highest, top)
        weight = jnp.exp(fresh - highest)
        total = jnp.sum(weight, axis=0, keepdims=True)
        mixed = mix(new_v[1, :, value_cols(head)], weight)
        for j in range(blocks_listed):
            source = src_ref[j, me]
            scale = jnp.exp(tops[j] - highest)
            total = total + scale * got_s[source, heads + head : heads + head + 1]
            mixed = mixed + scale * got_o[source, head * HD : (head + 1) * HD].astype(jnp.float32)
        put(1, head, mixed, total)

    for s in range(1, n):
        state_first(0, s).wait_send()
        state_first(1, s).wait_send()
        state_second(s).wait_send()
        for copy in part_copies(s):
            copy.wait_send()
    bc_copy().wait_send()
    q_over(0).wait_send()

    @pl.when(line < last)
    def _():
        q_right(0).wait_send()

    @pl.when(line > 0)
    def _():
        q_left(0).wait_send()

    for s in range(1, length):
        @pl.when(line - s >= 0)
        def _():
            q_over(-s).wait_send()

            @pl.when(line < last)
            def _():
                q_right(s).wait_send()

        @pl.when(line + s <= last)
        def _():
            q_over(s).wait_send()

            @pl.when(line > 0)
            def _():
                q_left(s).wait_send()

    for c in range(chunks):
        side_copy(c).wait_send()
        final_copy(c).wait_send()

        @pl.when(line < last)
        def _():
            right_copy(c).wait_send()

        @pl.when(line > 0)
        def _():
            left_copy(c).wait_send()


def local(
    queries,
    new_kv,
    cached_lookup_pairs,
    prefix_ssm,
    prefix_conv,
    pool_kv,
    pool_ssm,
    pool_conv,
    owner_id,
    readers,
    restore_src,
    restore_blk,
    state_src,
    ctx_blocks,
    mamba_x,
    mamba_z,
    mamba_dt,
    dt_bias,
    a_log,
    bypass_gain,
    conv_w,
    conv_b,
    w_bc,
):
    n = restore_src.shape[0]
    half_n = n // 2
    _, length, width = cached_lookup_pairs.shape
    _, states, channels = pool_ssm.shape
    _, _, new_len, q_width = queries.shape
    blocks, block_len = pool_kv.shape[1:3]
    part = length // 2 // KV_CHUNKS
    taps = conv_w.shape[0]
    assert part == channels // 2 // width * states and 2 * (taps - 1) <= 8
    kv = cached_lookup_pairs.reshape(2, KV_CHUNKS, part, width)
    fill = jnp.zeros((8 - 2 * (taps - 1), channels), pool_conv.dtype)
    conv = jnp.concatenate([pool_conv[0], prefix_conv[0], fill], axis=0)
    piece = (n, states + 8, channels // n)
    heads = width // (2 * HD)
    rows = Q_PER_KV * new_len
    chunks = KV_CHUNKS + 1
    bf16, f32 = jnp.bfloat16, jnp.float32
    smem = pl.BlockSpec(memory_space=pltpu.SMEM)
    any_spec = pl.BlockSpec(memory_space=pl.ANY)
    vmem = pl.BlockSpec(memory_space=pltpu.VMEM)
    stream = pltpu.VMEM((chunks, part, width), bf16)
    both = pltpu.VMEM((2, chunks, part, width), bf16)
    dma = pltpu.SemaphoreType.DMA
    return pl.pallas_call(
        lambda *refs: layer_kernel(n, *refs),
        in_specs=[smem] * 6 + [any_spec] * 16,
        out_specs=[vmem] * 2,
        out_shape=[
            jax.ShapeDtypeStruct((1, 2, new_len, q_width), bf16),
            jax.ShapeDtypeStruct((1, 2, new_len, channels), bf16),
        ],
        scratch_shapes=[
            pltpu.VMEM((n, new_len, q_width), bf16),
            pltpu.VMEM((blocks, block_len, width), bf16),
            pltpu.VMEM((n, heads * HD, rows), bf16),
            pltpu.VMEM((n, 8, rows), f32),
            pltpu.VMEM((n, heads * HD, rows), bf16),
            pltpu.VMEM((n, 8, rows), f32),
            pltpu.VMEM(piece, bf16),
            pltpu.VMEM(piece, bf16),
            pltpu.VMEM(piece, bf16),
            both,
        ]
        + [stream] * 5
        + [
            both,
            pltpu.VMEM((new_len, q_width), bf16),
            pltpu.VMEM((2, new_len, width), bf16),
        ]
        + [pltpu.VMEM((2, new_len, channels), bf16)] * 3
        + [
            pltpu.VMEM((1, channels), f32),
            pltpu.VMEM((states, channels), f32),
            pltpu.VMEM((1, channels), f32),
            pltpu.VMEM((taps, channels), f32),
            pltpu.VMEM((1, channels), f32),
            pltpu.VMEM((2 * states, channels), bf16),
            pltpu.VMEM((2, 8 + new_len, width), f32),
            pltpu.VMEM((2, new_len, channels), f32),
            pltpu.VMEM((2 * states, 128), f32),
            pltpu.VMEM((2 * states, 128), f32),
            pltpu.VMEM((2, new_len, 2 * states, HD), f32),
            pltpu.VMEM((2, new_len, width), f32),
            pltpu.VMEM((2, new_len, width), f32),
            pltpu.VMEM((2, new_len, width), f32),
            dma((32,)),
            dma((1,)),
            dma((3, n)),
            dma((3, n)),
            dma((2, n)),
            dma((2, n)),
            dma((3, n)),
            dma((3, n)),
            dma((4, chunks)),
            dma((4, chunks)),
            dma((1,)),
            dma((1,)),
        ],
        compiler_params=pltpu.CompilerParams(collective_id=0, has_side_effects=True),
        name="layer",
    )(
        owner_id, readers, jnp.swapaxes(restore_src, 0, 1), jnp.swapaxes(restore_blk, 0, 1), state_src, ctx_blocks,
        queries, new_kv, kv, prefix_ssm, pool_kv, pool_ssm, conv,
        mamba_x, mamba_z, mamba_dt, dt_bias[None], a_log, bypass_gain[None], conv_w, conv_b[None],
        jnp.swapaxes(w_bc, 0, 1),
    )


def placed_specs():
    return (
        P(("groups", "replica"), None, None, "channel"),
        P(("groups", "replica"), None, None, "channel"),
        P(("groups", "replica"), None, "channel"),
        P(("groups", "replica"), None, "channel"),
        P(("groups", "replica"), None, "channel"),
        P(("groups", "replica"), None, None, "channel"),
        P(("groups", "replica"), None, "channel"),
        P(("groups", "replica"), None, "channel"),
        P("groups"),
        P(("groups", "replica")),
        P("groups", None),
        P("groups", None),
        P("groups"),
        P(("groups", "replica")),
        P(("groups", "replica"), None, None, "channel"),
        P(("groups", "replica"), None, None, "channel"),
        P(("groups", "replica"), None, None, "channel"),
        P("channel"),
        P(None, "channel"),
        P("channel"),
        P(None, "channel"),
        P("channel"),
        P("channel", None),
    )


def solution(mesh):
    return jax.shard_map(
        local,
        mesh=mesh,
        in_specs=placed_specs(),
        out_specs=(
            P(("groups", "replica"), None, None, "channel"),
            P(("groups", "replica"), None, None, "channel"),
        ),
        check_vma=False,
    )
```

time: 114 us -> 88.8 us (0.78)
  waiting for transfers between devices: 17.7 us -> 0 us
  Pallas kernels: 72.5 us -> 81.8 us
  blocking collectives: 4.63 us -> 0 us
  local copies, waits for them, and re-layouts: 6.79 us -> 2.6 us
  other arithmetic: 5.5 us -> 1.48 us
  starting transfers between devices: 3.75 us -> 0 us
    all_to_all x1 -> x0, waiting for transfers between devices: 17.7 us -> none  [local(): lax.all_to_all(send_kv[:, None], 'replica', split_axis=0, concat_axis=1,...]
    pallas_call x5 -> x1, Pallas kernels: 72.5 us -> 81.8 us  [local(): pl.pallas_call(lambda *refs: layer_kernel(n, *refs), in_specs=[smem] * 6...]
    psum x1 -> x0, blocking collectives: 4.63 us -> none  [local(): state_bc = lax.psum(partial_bc, 'channel')]
    all_to_all x1 -> x0, starting transfers between devices: 3.75 us -> none  [local(): lax.all_to_all(send_kv[:, None], 'replica', split_axis=0, concat_axis=1,...]
    gather x1 -> x0, local copies, waits for them, and re-layouts: 2.02 us -> none  [local(): send_kv = jnp.take(pool_kv[0], picked, axis=0, mode='clip')]
    broadcast_in_dim x1 -> x0, other arithmetic: 1.63 us -> none  [local(): return (jnp.stack([fresh_out, resumed_out])[None], mamba_out)]
    concatenate x3 -> x1, other arithmetic: 3.05 us -> 1.48 us  [local(): conv = jnp.concatenate([pool_conv[0], prefix_conv[0], fill], axis=0)]
    unnamed x14 -> x4, local copies, waits for them, and re-layouts: 2.78 us -> 2.52 us
  transfers between devices with their start and end apart: 1 -> 0, of which waited for: 1 -> 0; matrix products, arithmetic and copies ran while one was open for 2% -> 0% of each run, Pallas kernels for 18% -> 0%
where the time goes in v1:
time: 88.8 us; the launch traced here: 88.5 us
  Pallas kernels  81.8 us (92%)
  local copies, waits for them, and re-layouts  2.6 us (3%)
  between operations  2.59 us (3%)
  other arithmetic  1.48 us (2%)
    pallas_call x1, Pallas kernels, local(): pl.pallas_call(lambda *refs: layer_kernel(n, *refs), in_specs=[smem] * 6...  81.8 us
    unnamed x4, local copies, waits for them, and re-layouts  2.52 us

profile of v1, /device:TPU:0, one launch (start us, length us, event | category | flops | bytes accessed | tf_op | source)
XLA Modules:
  0.0 88.5 jit_solution(17297080961317387156)
XLA Ops:
  2.6 0.1 pad.2.clone
  2.7 1.5 %maximum_maximum_fusion.refs_12_ = bf16[8,4096]{1,0:T(8,128)(2,1)} fusion(bf16[3,4096]{1,0:T(4,128)(2,1)} %bitcast.11, bf16[3,4096]{1,0:T(4,128)(2,1)} %bitcast.12, bf16[8]{0:T(256)(128)(2,1)S(1)} %pad.2.clone), kind=kLoop, calls=%fused_computation | loop fusion | flops 196608 | bytes 114704 | tf_op jit(solution)/shard_map/concatenate | solution.py:566
  4.1 81.8 %layer.1 = (bf16[1,2,32,2048]{3,2,1,0:T(8,128)(2,1)}, bf16[1,2,32,4096]{3,2,1,0:T(8,128)(2,1)}) custom-call(s32[1]{0:T(128)S(6)} %copy.27.refs_0_, s32[1]{0:T(128)S(6)} %copy.28.refs_1_, s32[4,8]{1,0:T(4,128)} %bitcast.16, s32[4,8]{1,0:T(4,128)} %bitcast.17, s32[8]{0:T(128)} %refs_4_.1, s32[1]{0:T(128)S(6)} %copy.29.refs_5_, ...), custom_call_target="tpu_custom_call" | custom-call | tf_op jit(solution)/shard_map/layer/pallas_call | solution.py:578
  86.0 0.0 copy-start
  86.0 1.7 %copy.30 = bf16[1,2,32,2048]{3,2,1,0:T(8,128)(2,1)} copy(bf16[1,2,32,2048]{3,2,1,0:T(8,128)(2,1)} %get-tuple-element.4) | data formatting | bytes 524288
  87.7 0.0 copy-done
  87.7 0.8 copy.31
  (1 shorter events, 0.0 us)
Async XLA Ops:
  86.0 1.7 %copy-start = (bf16[1,2,32,4096]{3,2,1,0:T(8,128)(2,1)S(1)}, bf16[1,2,32,4096]{3,2,1,0:T(8,128)(2,1)}, u32[]{:S(2)}) copy-start(bf16[1,2,32,4096]{3,2,1,0:T(8,128)(2,1)} %get-tuple-element.5) | copy-start | bytes 1572868

commit v2 on v1

--- a/solution.py
+++ b/solution.py
@@ -7,7 +7,15 @@
 
 HD = 128
 Q_PER_KV = 8
-KV_CHUNKS = 8
+KV_CHUNKS = 16
+SKEW = 4
+AHEAD = 6
+RELAYS = (0.02, 0.3)
+OVERS = (0.34, 0.6)
+KEEPS = (0.65, 0.95)
+SIGNALS = (0.2, 0.36)
+SCANS = (0.42, 0.95)
+OUT_OF_REACH = -1e30
 MESH = pl.DeviceIdType.MESH
 
 
@@ -23,35 +31,37 @@
 
 def layer_kernel(
     n,
-    owner_ref, read_ref, src_ref, blk_ref, holder_ref, ctx_ref,
-    q_ref, new_ref, kv_ref, pssm_ref, pool_ref, ossm_ref, conv_ref,
+    owner_any, read_any, src_any, blk_any, holder_any, ctx_any,
+    q_ref, new_ref, kv_ref, pssm_ref, pool_ref, ossm_ref, oconv_ref, pconv_ref,
     x_ref, z_ref, dt_ref, bias_ref, alog_ref, gain_ref, cw_ref, cb_ref, wbc_ref,
     att_ref, mam_ref,
-    q_all, pool_v, part_o, part_s, got_o, got_s,
+    owner_ref, read_ref, src_ref, blk_ref, holder_ref, ctx_ref, oconv_v, pconv_v, conv_f, conv_ref,
+    q_all, pool_v, over_o, over_s, side_o, side_s, keep_o, keep_s, got_o, got_s,
     cand, piece, states,
     own, side, rightward, leftward, to_right, to_left, shared,
     q0_v, new_v, x_v, z_v, dt_v, bias_v, alog_v, gain_v, cw_v, cb_v, wbc_v,
     pad, sig, bc_mine, bc_theirs, spread, step_buf, push_buf, scan_buf,
-    load_sems, own_sems, st_send, st_recv, p_send, p_recv, q_send, q_recv,
+    load_sems, st_send, st_recv, p_send, p_recv, q_send, q_recv,
     ch_send, ch_recv, bc_send, bc_recv,
 ):
     me = lax.axis_index("replica")
     core = lax.axis_index("channel")
     line, half = me // 2, lax.rem(me, 2)
     length = n // 2
-    last = length - 1
+    last = last_line = length - 1
     partner = line * 2 + 1 - half
-    owner = owner_ref[0]
-    owner_line = owner // 2
-    reading = read_ref[0] > 0
     states_n, channels = alog_v.shape
     new_len = q0_v.shape[0]
     heads = new_v.shape[2] // (2 * HD)
     rows = Q_PER_KV * new_len
-    chunks, _, width = side.shape
+    chunks, part, width = side.shape
     piece_w = cand.shape[2]
     per = width // piece_w
     wide = channels // width
+    per_half = wide // 2
+    lead = per_half * states_n // part
+    per_part = part // states_n
+    taps = cw_v.shape[0]
     blocks_listed = src_ref.shape[0]
 
     barrier = pltpu.get_barrier_semaphore()
@@ -70,21 +80,26 @@
         return copy
 
     load_q = load(q_ref.at[0, 1], q_all.at[me])
-    load_kv = load(kv_ref, own.at[:, pl.ds(1, chunks - 1)])
+    load_rows = [load(oconv_ref.at[0], oconv_v), load(pconv_ref.at[0], pconv_v)]
+    load_scalars = [
+        load(owner_any, owner_ref), load(read_any, read_ref), load(src_any, src_ref),
+        load(blk_any, blk_ref), load(holder_any, holder_ref), load(ctx_any, ctx_ref),
+    ]
+    load_kv = load(kv_ref, own.at[:, pl.ds(lead, chunks - lead)])
     load_ssm = []
-    per_half = wide // 2
     for g in range(wide):
         load_ssm.append(
             load(
                 pssm_ref.at[0, :, pl.ds(g * width, width)],
-                own.at[g // per_half, 0, pl.ds(g % per_half * states_n, states_n)],
+                own.at[
+                    g // per_half,
+                    g % per_half * states_n // part,
+                    pl.ds(g % per_half * states_n % part, states_n),
+                ],
             )
         )
     mine = pl.ds(pl.multiple_of(me * piece_w, piece_w), piece_w)
-    load_cand = [
-        load(ossm_ref.at[0, :, mine], cand.at[me, pl.ds(0, states_n)]),
-        load(conv_ref.at[:, mine], cand.at[me, pl.ds(states_n, 8)]),
-    ]
+    load_cand = load(ossm_ref.at[0, :, mine], cand.at[me, pl.ds(0, states_n)])
     load_pool = load(pool_ref.at[0], pool_v)
     load_conv = [load(x_ref.at[0], x_v), load(cw_ref, cw_v), load(cb_ref, cb_v), load(wbc_ref, wbc_v)]
     load_scan = [
@@ -102,39 +117,51 @@
     def peer_of(s):
         return lax.rem(me + s, n)
 
+    for copy in load_rows + load_scalars:
+        copy.wait()
+    conv_f[...] = jnp.zeros_like(conv_f)
+    conv_f[: taps - 1] = oconv_v[...].astype(jnp.float32)
+    conv_f[taps - 1 : 2 * taps - 2] = pconv_v[...].astype(jnp.float32)
+    conv_f[2 * taps - 2 : 2 * taps - 1] = jnp.full((1, channels), ctx_ref[0].astype(jnp.float32))
+    conv_ref[...] = conv_f[...].astype(conv_ref.dtype)
+    cand[me, states_n:] = conv_ref[:, mine]
+    owner = owner_ref[0]
+    owner_line = owner // 2
+    reading = read_ref[0] > 0
     load_q.wait()
     pl.semaphore_wait(barrier, n)
 
-    def q_right(s):
-        item = q_all.at[(line - s) * 2 + half]
-        return remote(item, item, q_send.at[0, s], q_recv.at[0, s], lax.rem(me + 2, n))
-
-    def q_left(s):
-        item = q_all.at[(line + s) * 2 + half]
-        return remote(item, item, q_send.at[1, s], q_recv.at[1, s], lax.rem(me + n - 2, n))
-
-    def q_from_left(s):
-        item = q_all.at[(line - s) * 2 + half]
-        return remote(item, item, q_send.at[0, s - 1], q_recv.at[0, s - 1], partner)
-
-    def q_from_right(s):
-        item = q_all.at[(line + s) * 2 + half]
-        return remote(item, item, q_send.at[1, s - 1], q_recv.at[1, s - 1], partner)
-
-    def q_over(s):
-        item = q_all.at[(line + s) * 2 + half]
-        index = length - 1 + s
-        return remote(item, item, q_send.at[2, index], q_recv.at[2, index], partner)
-
-    @pl.when(line < last)
-    def _():
-        q_right(0).start()
-
-    @pl.when(line > 0)
-    def _():
-        q_left(0).start()
-
-    q_over(0).start()
+    def q_item(s, kind):
+        return q_all.at[(line + s) * 2 + (half if kind == 0 else 1 - half)]
+
+    def q_over():
+        item = q_item(0, 0)
+        return remote(item, item, q_send.at[4, 0], q_recv.at[4, 0], partner)
+
+    def q_right(s, kind):
+        item = q_item(-s, kind)
+        return remote(item, item, q_send.at[kind, s], q_recv.at[kind, s], lax.rem(me + 2, n))
+
+    def q_left(s, kind):
+        item = q_item(s, kind)
+        return remote(item, item, q_send.at[2 + kind, s], q_recv.at[2 + kind, s], lax.rem(me + n - 2, n))
+
+    def q_arrival(s, kind, leftward_bound):
+        item = q_item(s if leftward_bound else -s, kind)
+        row = kind + (2 if leftward_bound else 0)
+        return remote(item, item, q_send.at[row, s - 1], q_recv.at[row, s - 1], partner)
+
+    def q_start(kind):
+        @pl.when(line < last)
+        def _():
+            q_right(0, kind).start()
+
+        @pl.when(line > 0)
+        def _():
+            q_left(0, kind).start()
+
+    q_over().start()
+    q_start(0)
 
     def state_first(kind, s):
         peer = peer_of(s)
@@ -174,9 +201,10 @@
     near, far = jnp.minimum(line, last - line), jnp.maximum(line, last - line)
 
     def spread_step(t):
-        if t + 1 < chunks:
-            side_copy(t + 1).start()
-        c_near, c_right, c_left, c_far = t - near, t - line, t - (last - line), t - far
+        if t + AHEAD < chunks:
+            side_copy(t + AHEAD).start()
+        c_near, c_far = t - SKEW * near, t - SKEW * far
+        c_right, c_left = t - SKEW * line, t - SKEW * (last - line)
 
         @pl.when((c_near >= 0) & (c_near < chunks))
         def _():
@@ -216,23 +244,25 @@
     load_kv.wait()
     for copy in load_ssm:
         copy.wait()
-    side_copy(0).start()
-
-    for copy in load_cand:
-        copy.wait()
-    for s in range(1, n):
-        state_first(0, s).wait_recv()
-        state_first(1, s).wait_recv()
-    conv_row = lax.broadcasted_iota(jnp.int32, (8, piece_w), 0)
-    shared_conv = cand[owner, states_n:].astype(jnp.float32)
-    for d in range(n):
-        holder = holder_ref[d]
-        piece[d, :states_n] = cand[holder, :states_n]
-        stored_conv = cand[holder, states_n:].astype(jnp.float32)
-        piece[d, states_n:] = jnp.where(conv_row < 3, stored_conv, shared_conv).astype(piece.dtype)
-    for s in range(1, n):
-        state_second(s).start()
-    states[me] = piece[me]
+    for c in range(AHEAD):
+        side_copy(c).start()
+
+    def state_unit():
+        load_cand.wait()
+        for s in range(1, n):
+            state_first(0, s).wait_recv()
+            state_first(1, s).wait_recv()
+        conv_row = lax.broadcasted_iota(jnp.int32, (8, piece_w), 0)
+        shared_conv = cand[owner, states_n:].astype(jnp.float32)
+        for d in range(n):
+            holder = holder_ref[d]
+            piece[d, :states_n] = cand[holder, :states_n]
+            stored_conv = cand[holder, states_n:].astype(jnp.float32)
+            merged = jnp.where(conv_row < taps - 1, stored_conv, shared_conv)
+            piece[d, states_n:] = merged.astype(piece.dtype)
+        for s in range(1, n):
+            state_second(s).start()
+        states[me] = piece[me]
 
     def query_rows(load_piece, head):
         return jnp.concatenate(
@@ -245,69 +275,84 @@
     def value_cols(head):
         return slice((2 * head + 1) * HD, (2 * head + 2) * HD)
 
-    def partial(d, out_o, out_s):
-        block = jnp.int32(0)
+    def partial(d):
+        block, slot = jnp.int32(0), jnp.int32(blocks_listed * n)
         for j in range(blocks_listed):
-            block = block + jnp.where(src_ref[j, d] == me, blk_ref[j, d], 0)
+            listed = src_ref[j, d] == me
+            block = block + jnp.where(listed, blk_ref[j, d], 0)
+            slot = jnp.where(listed, j, slot)
+        held = cand[d, states_n:, :HD].astype(jnp.float32)[2 * taps - 2 : 2 * taps - 1]
+        held = jnp.concatenate([held] * (rows // HD), axis=1)
+        live = slot.astype(jnp.float32) < held
+        results = []
         for head in range(heads):
             query = query_rows(lambda at: q_all[d, :, at : at + HD], head)
             score = scores_of(pool_v[block, :, key_cols(head)], query)
             highest = jnp.max(score, axis=0, keepdims=True)
             weight = jnp.exp(score - highest)
             mixed = mix(pool_v[block, :, value_cols(head)], weight)
-            out_o[head * HD : (head + 1) * HD] = mixed.astype(jnp.bfloat16)
-            out_s[head : head + 1] = highest
-            out_s[heads + head : heads + head + 1] = jnp.sum(weight, axis=0, keepdims=True)
-
-    def part_copies(s):
-        peer = peer_of(s)
+            total = jnp.sum(weight, axis=0, keepdims=True)
+            results.append((mixed, jnp.where(live, highest, OUT_OF_REACH), total))
+        return results
+
+    def store(out_o, out_s, head, mixed, highest, total):
+        out_o[head * HD : (head + 1) * HD] = mixed.astype(jnp.bfloat16)
+        out_s[head : head + 1] = highest
+        out_s[heads + head : heads + head + 1] = total
+
+    def line_of(s):
+        return lax.rem(line + s, length)
+
+    def over_copies(s):
+        at = line_of(s)
         return (
-            remote(part_o.at[peer], got_o.at[me], p_send.at[0, s], p_recv.at[0, s], peer),
-            remote(part_s.at[peer], got_s.at[me], p_send.at[1, s], p_recv.at[1, s], peer),
+            remote(over_o.at[at], side_o.at[at], p_send.at[0, s], p_recv.at[0, s], partner),
+            remote(over_s.at[at], side_s.at[at], p_send.at[1, s], p_recv.at[1, s], partner),
+        )
+
+    def keep_copies(s):
+        at = line_of(s)
+        peer = at * 2 + half
+        return (
+            remote(keep_o.at[at], got_o.at[line], p_send.at[2, s], p_recv.at[2, s], peer),
+            remote(keep_s.at[at], got_s.at[line], p_send.at[3, s], p_recv.at[3, s], peer),
         )
 
     def relay_unit(s):
         def go():
-            @pl.when(line - s >= 0)
-            def _():
-                q_from_left(s).wait_recv()
-
-                @pl.when(line < last)
+            if s == 0:
+                q_over().wait_recv()
+                q_start(1)
+                return
+            for kind in range(2):
+                @pl.when(line - s >= 0)
                 def _():
-                    q_right(s).start()
-
-                q_over(-s).start()
-
-            @pl.when(line + s <= last)
-            def _():
-                q_from_right(s).wait_recv()
-
-                @pl.when(line > 0)
+                    q_arrival(s, kind, False).wait_recv()
+
+                    @pl.when(line < last)
+                    def _():
+                        q_right(s, kind).start()
+
+                @pl.when(line + s <= last)
                 def _():
-                    q_left(s).start()
-
-                q_over(s).start()
+                    q_arrival(s, kind, True).wait_recv()
+
+                    @pl.when(line > 0)
+                    def _():
+                        q_left(s, kind).start()
 
         return go
 
-    def gathered():
-        for s in range(-last, length):
-            @pl.when((line + s >= 0) & (line + s <= last))
-            def _():
-                q_over(s).wait_recv()
-
-        load_pool.wait()
-
-    def visit_unit(low, high):
+    def over_unit(low, high):
         def go():
-            if low == 1:
-                gathered()
-                partial(me, got_o.at[me], got_s.at[me])
+            if low == 0:
+                load_pool.wait()
 
             def body(s, carry):
-                peer = peer_of(s)
-                partial(peer, part_o.at[peer], part_s.at[peer])
-                for copy in part_copies(s):
+                at = line_of(s)
+                for head, result in enumerate(partial(at * 2 + 1 - half)):
+                    store(over_o.at[at], over_s.at[at], head, *result)
+                for copy in over_copies(s):
                     copy.start()
                 return carry
 
@@ -315,7 +360,35 @@
 
         return go
 
-    taps = cw_v.shape[0]
+    def keep_row(s, out_o, out_s):
+        at = line_of(s)
+        results = partial(at * 2 + half)
+        for copy in over_copies(s):
+            copy.wait_recv()
+        for head, (mixed, highest, total) in enumerate(results):
+            theirs = side_s[at, head : head + 1]
+            both = jnp.maximum(highest, theirs)
+            ours, theirs = jnp.exp(highest - both), jnp.exp(theirs - both)
+            mixed = ours * mixed + theirs * side_o[at, head * HD : (head + 1) * HD].astype(jnp.float32)
+            total = ours * total + theirs * side_s[at, heads + head : heads + head + 1]
+            store(out_o, out_s, head, mixed, both, total)
+
+    def keep_unit(low, high):
+        def go():
+            def body(s, carry):
+                at = line_of(s)
+                keep_row(s, keep_o.at[at], keep_s.at[at])
+                for copy in keep_copies(s):
+                    copy.start()
+                return carry
+
+            lax.fori_loop(low, high, body, 0)
+
+        return go
+
+    def own_unit():
+        keep_row(0, got_o.at[line], got_s.at[line])
+
     base = 8 - (taps - 1)
 
     def lanes(i):
@@ -376,7 +449,8 @@
                         spread[r, t] = jnp.broadcast_to(total[:, at : at + 1], spread.shape[2:])
                 for copy in load_scan:
                     copy.wait()
-                final_copy(0).wait_recv()
+                for c in range(lead):
+                    final_copy(c).wait_recv()
 
             def body(i, carry):
                 decay = -jnp.exp(alog_v[:, lanes(i)])
@@ -385,8 +459,9 @@
                     step = jnp.maximum(x, 0.0) + jnp.log1p(jnp.exp(-jnp.abs(x)))
                     step_buf[r] = step
                     push_buf[r] = step * sig[r, :, lanes(i)]
-                group = pl.ds(pl.multiple_of(lax.rem(i, per_half) * states_n, states_n), states_n)
-                first = shared[i // per_half, 0, group].astype(jnp.float32)
+                place = lax.rem(i, per_half)
+                group = pl.ds(pl.multiple_of(lax.rem(place, per_part) * states_n, states_n), states_n)
+                first = shared[i // per_half, place // per_part, group].astype(jnp.float32)
                 hidden = [jnp.where(reading, first, 0.0), stored(i)[:states_n]]
                 tiles = width // HD
                 for t in range(new_len):
@@ -408,21 +483,30 @@
 
         return go
 
-    visits = [1 + (n - 1) * k // 2 for k in range(3)]
-    units = [relay_unit(s) for s in range(1, length)]
-    units += [visit_unit(low, high) for low, high in zip(visits[:-1], visits[1:])]
-    units += [signal_unit(0, wide // 2), signal_unit(wide // 2, wide)]
-    units += [scan_unit(k * wide // 4, (k + 1) * wide // 4) for k in range(4)]
-    steps = chunks + length - 1
-    done = 0
+    def spaced(span, units):
+        gap = (span[1] - span[0]) / max(len(units) - 1, 1)
+        return [(span[0] + gap * k, unit) for k, unit in enumerate(units)]
+
+    def grouped(make, low, high, most):
+        count = min(most, high - low)
+        edges = [low + (high - low) * k // count for k in range(count + 1)]
+        return [make(a, b) for a, b in zip(edges[:-1], edges[1:])]
+
+    relays = [relay_unit(s) for s in range(length)]
+    plan = spaced(RELAYS, relays[:2] + [state_unit] + relays[2:])
+    plan += spaced(OVERS, grouped(over_unit, 0, length, 4))
+    plan += spaced(KEEPS, grouped(keep_unit, 1, length, 3) + [own_unit])
+    plan += spaced(SIGNALS, grouped(signal_unit, 0, wide, 2))
+    steps = chunks + SKEW * last_line
+    ready = (SKEW * last_line + lead + 1) / steps
+    plan += spaced((max(SCANS[0], ready), max(SCANS[1], ready)), grouped(scan_unit, 0, wide, 8))
+    plan.sort(key=lambda entry: entry[0])
     for t in range(steps):
         spread_step(t)
-        until = (t + 1) * len(units) // steps
-        for unit in units[done:until]:
-            unit()
-        done = until
-
-    for c in range(1, chunks):
+        while plan and plan[0][0] * steps <= t + 1:
+            plan.pop(0)[1]()
+
+    for c in range(lead, chunks):
         final_copy(c).wait_recv()
     for copy in load_att:
         copy.wait()
@@ -444,7 +528,7 @@
         highest = jnp.max(fresh, axis=0, keepdims=True)
         scores = []
         for h in range(2):
-            keys = shared[h, 1:, :, key_cols(head)].reshape(-1, HD)
+            keys = shared[h, lead:, :, key_cols(head)].reshape(-1, HD)
             score = jnp.where(reading, scores_of(keys, query), -jnp.inf)
             highest = jnp.maximum(highest, jnp.max(score, axis=0, keepdims=True))
             scores.append(score)
@@ -454,65 +538,47 @@
         for h in range(2):
             weight = jnp.exp(scores[h] - highest)
             total = total + jnp.sum(weight, axis=0, keepdims=True)
-            mixed = mixed + mix(shared[h, 1:, :, value_cols(head)].reshape(-1, HD), weight)
+            mixed = mixed + mix(shared[h, lead:, :, value_cols(head)].reshape(-1, HD), weight)
         put(0, head, mixed, total)
 
-    for s in range(1, n):
-        for copy in part_copies(s):
+    for s in range(1, length):
+        for copy in keep_copies(s):
             copy.wait_recv()
-    live = ctx_ref[0]
     for head in range(heads):
         query = query_rows(lambda at: q_all[me, :, at : at + HD], head)
         fresh = causal(scores_of(new_v[1, :, key_cols(head)], query))
         highest = jnp.max(fresh, axis=0, keepdims=True)
-        tops = []
-        for j in range(blocks_listed):
-            top = jnp.where(j < live, got_s[src_ref[j, me], head : head + 1], -jnp.inf)
-            tops.append(top)
-            highest = jnp.maximum(highest, top)
+        for at in range(length):
+            highest = jnp.maximum(highest, got_s[at, head : head + 1])
         weight = jnp.exp(fresh - highest)
         total = jnp.sum(weight, axis=0, keepdims=True)
         mixed = mix(new_v[1, :, value_cols(head)], weight)
-        for j in range(blocks_listed):
-            source = src_ref[j, me]
-            scale = jnp.exp(tops[j] - highest)
-            total = total + scale * got_s[source, heads + head : heads + head + 1]
-            mixed = mixed + scale * got_o[source, head * HD : (head + 1) * HD].astype(jnp.float32)
+        for at in range(length):
+            scale = jnp.exp(got_s[at, head : head + 1] - highest)
+            total = total + scale * got_s[at, heads + head : heads + head + 1]
+            mixed = mixed + scale * got_o[at, head * HD : (head + 1) * HD].astype(jnp.float32)
         put(1, head, mixed, total)
 
     for s in range(1, n):
         state_first(0, s).wait_send()
         state_first(1, s).wait_send()
         state_second(s).wait_send()
-        for copy in part_copies(s):
+    bc_copy().wait_send()
+    q_over().wait_send()
+    for s in range(length):
+        for copy in over_copies(s):
             copy.wait_send()
-    bc_copy().wait_send()
-    q_over(0).wait_send()
-
-    @pl.when(line < last)
-    def _():
-        q_right(0).wait_send()
-
-    @pl.when(line > 0)
-    def _():
-        q_left(0).wait_send()
-
-    for s in range(1, length):
-        @pl.when(line - s >= 0)
-        def _():
-            q_over(-s).wait_send()
-
-            @pl.when(line < last)
+        if s > 0:
+            for copy in keep_copies(s):
+                copy.wait_send()
+        for kind in range(2):
+            @pl.when((line - s >= 0) & (line < last))
             def _():
-                q_right(s).wait_send()
-
-        @pl.when(line + s <= last)
-        def _():
-            q_over(s).wait_send()
-
-            @pl.when(line > 0)
+                q_right(s, kind).wait_send()
+
+            @pl.when((line + s <= last) & (line > 0))
             def _():
-                q_left(s).wait_send()
+                q_left(s, kind).wait_send()
 
     for c in range(chunks):
         side_copy(c).wait_send()
@@ -560,16 +626,14 @@
     blocks, block_len = pool_kv.shape[1:3]
     part = length // 2 // KV_CHUNKS
     taps = conv_w.shape[0]
-    assert part == channels // 2 // width * states and 2 * (taps - 1) <= 8
+    lead = channels // 2 // width * states // part
+    assert lead * part == channels // 2 // width * states and part % states == 0 and 2 * (taps - 1) < 8
     kv = cached_lookup_pairs.reshape(2, KV_CHUNKS, part, width)
-    fill = jnp.zeros((8 - 2 * (taps - 1), channels), pool_conv.dtype)
-    conv = jnp.concatenate([pool_conv[0], prefix_conv[0], fill], axis=0)
     piece = (n, states + 8, channels // n)
     heads = width // (2 * HD)
     rows = Q_PER_KV * new_len
-    chunks = KV_CHUNKS + 1
+    chunks = KV_CHUNKS + lead
     bf16, f32 = jnp.bfloat16, jnp.float32
-    smem = pl.BlockSpec(memory_space=pltpu.SMEM)
     any_spec = pl.BlockSpec(memory_space=pl.ANY)
     vmem = pl.BlockSpec(memory_space=pltpu.VMEM)
     stream = pltpu.VMEM((chunks, part, width), bf16)
@@ -577,19 +641,26 @@
     dma = pltpu.SemaphoreType.DMA
     return pl.pallas_call(
         lambda *refs: layer_kernel(n, *refs),
-        in_specs=[smem] * 6 + [any_spec] * 16,
+        in_specs=[any_spec] * 23,
         out_specs=[vmem] * 2,
         out_shape=[
             jax.ShapeDtypeStruct((1, 2, new_len, q_width), bf16),
             jax.ShapeDtypeStruct((1, 2, new_len, channels), bf16),
         ],
         scratch_shapes=[
+            pltpu.SMEM((1,), jnp.int32),
+            pltpu.SMEM((1,), jnp.int32),
+            pltpu.SMEM((restore_src.shape[1], n), jnp.int32),
+            pltpu.SMEM((restore_src.shape[1], n), jnp.int32),
+            pltpu.SMEM((n,), jnp.int32),
+            pltpu.SMEM((1,), jnp.int32),
+            pltpu.VMEM((taps - 1, channels), bf16),
+            pltpu.VMEM((taps - 1, channels), bf16),
+            pltpu.VMEM((8, channels), f32),
+            pltpu.VMEM((8, channels), bf16),
             pltpu.VMEM((n, new_len, q_width), bf16),
             pltpu.VMEM((blocks, block_len, width), bf16),
-            pltpu.VMEM((n, heads * HD, rows), bf16),
-            pltpu.VMEM((n, 8, rows), f32),
-            pltpu.VMEM((n, heads * HD, rows), bf16),
-            pltpu.VMEM((n, 8, rows), f32),
+            *[pltpu.VMEM((half_n, heads * HD, rows), bf16), pltpu.VMEM((half_n, 8, rows), f32)] * 4,
             pltpu.VMEM(piece, bf16),
             pltpu.VMEM(piece, bf16),
             pltpu.VMEM(piece, bf16),
@@ -617,14 +688,13 @@
             pltpu.VMEM((2, new_len, width), f32),
             pltpu.VMEM((2, new_len, width), f32),
             pltpu.VMEM((2, new_len, width), f32),
-            dma((32,)),
-            dma((1,)),
+            dma((48,)),
             dma((3, n)),
             dma((3, n)),
-            dma((2, n)),
-            dma((2, n)),
-            dma((3, n)),
-            dma((3, n)),
+            dma((4, half_n)),
+            dma((4, half_n)),
+            dma((5, half_n)),
+            dma((5, half_n)),
             dma((4, chunks)),
             dma((4, chunks)),
             dma((1,)),
@@ -634,7 +704,7 @@
         name="layer",
     )(
         owner_id, readers, jnp.swapaxes(restore_src, 0, 1), jnp.swapaxes(restore_blk, 0, 1), state_src, ctx_blocks,
-        queries, new_kv, kv, prefix_ssm, pool_kv, pool_ssm, conv,
+        queries, new_kv, kv, prefix_ssm, pool_kv, pool_ssm, pool_conv, prefix_conv,
         mamba_x, mamba_z, mamba_dt, dt_bias[None], a_log, bypass_gain[None], conv_w, conv_b[None],
         jnp.swapaxes(w_bc, 0, 1),
     )

time: 88.8 us -> 73.3 us (0.83)
  Pallas kernels: 81.8 us -> 68 us
  other arithmetic: 1.48 us -> 0 us
    pallas_call x1, Pallas kernels: 81.8 us -> 68 us  [local(): pl.pallas_call(lambda *refs: layer_kernel(n, *refs), in_specs=[any_spec]...]
    concatenate x1 -> x0, other arithmetic: 1.48 us -> none  [local(): conv = jnp.concatenate([pool_conv[0], prefix_conv[0], fill], axis=0)]
where the time goes in v2:
time: 73.3 us; the launch traced here: 73.1 us
  Pallas kernels  68 us (93%)
  between operations  2.59 us (4%)
  local copies, waits for them, and re-layouts  2.52 us (3%)
    pallas_call x1, Pallas kernels, local(): pl.pallas_call(lambda *refs: layer_kernel(n, *refs), in_specs=[any_spec]...  68 us
    unnamed x4, local copies, waits for them, and re-layouts  2.52 us

profile of v2, /device:TPU:0, one launch (start us, length us, event | category | flops | bytes accessed | tf_op | source)
XLA Modules:
  0.0 73.1 jit_solution(9062345349833799517)
XLA Ops:
  2.6 68.0 %layer.1 = (bf16[1,2,32,2048]{3,2,1,0:T(8,128)(2,1)}, bf16[1,2,32,4096]{3,2,1,0:T(8,128)(2,1)}) custom-call(s32[1]{0:T(128)S(6)} %copy.27.refs_0_, s32[1]{0:T(128)S(6)} %copy.28.refs_1_, s32[4,8]{1,0:T(4,128)} %bitcast.12, s32[4,8]{1,0:T(4,128)} %bitcast.13, s32[8]{0:T(128)} %refs_4_.1, s32[1]{0:T(128)S(6)} %copy.29.refs_5_, ...), custom_call_target="tpu_custom_call" | custom-call | tf_op jit(solution)/shard_map/layer/pallas_call | solution.py:642
  70.6 0.0 copy-start
  70.6 1.7 %copy.30 = bf16[1,2,32,2048]{3,2,1,0:T(8,128)(2,1)} copy(bf16[1,2,32,2048]{3,2,1,0:T(8,128)(2,1)} %get-tuple-element.4) | data formatting | bytes 524288
  72.3 0.0 copy-done
  72.3 0.8 %copy.31 = bf16[1,2,32,4096]{3,2,1,0:T(8,128)(2,1)} copy(bf16[1,2,32,4096]{3,2,1,0:T(8,128)(2,1)S(1)} %copy-done) | data formatting | bytes 1048576
Async XLA Ops:
  70.6 1.7 %copy-start = (bf16[1,2,32,4096]{3,2,1,0:T(8,128)(2,1)S(1)}, bf16[1,2,32,4096]{3,2,1,0:T(8,128)(2,1)}, u32[]{:S(2)}) copy-start(bf16[1,2,32,4096]{3,2,1,0:T(8,128)(2,1)} %get-tuple-element.5) | copy-start | bytes 1572868
